TPU v7x, 512 devices: a whole 4x4x16 slice. The times are simulated.
512 devices in a mesh: cuts: 128 (over z, x, core), stem: 4 (over y).
Axes of the slice: x: 4, y: 4, z: 16, core: 2. Of those that a mesh axis runs over, the one named last changes fastest.
Arguments:
- stem_tensor: bfloat16 [8, 64, 1024], P('stem'), may hold values from -6 to 6
- mid_tensors: bfloat16 [8192, 512, 128], P(('cuts', 'stem')), may hold values from -0.1875 to 0.1875
- right_tensors: bfloat16 [8, 8192, 64, 128], P(None, ('cuts', 'stem')), may hold values from -0.001953125 to 0.001953125
Outputs:
- amplitudes: float32 [8192], P('cuts')
All inputs are finite; a program needn't handle non-finite values.
Results may differ from a plain program's by a relative error of at most 0.0029.
Values may be sent and summed in bfloat16 or wider, within the bound.
A program may use at most 64 MiB of HBM per device.

v0:
```python
import jax
import jax.numpy as jnp
from jax import lax
from jax.sharding import PartitionSpec as P


def widen(tensor):
    half_width = tensor.shape[-1] // 2
    real_part = tensor[..., :half_width]
    imag_part = tensor[..., half_width:]
    upper_rows = jnp.concatenate([real_part, imag_part], axis=-1)
    lower_rows = jnp.concatenate([-imag_part, real_part], axis=-1)
    return jnp.concatenate([upper_rows, lower_rows], axis=-2)


def on_device(stem_tensor, mid_tensors, right_tensors):
    local_blocks, rows_a, width = stem_tensor.shape
    cols_b = right_tensors.shape[-1]
    widened = jnp.moveaxis(widen(mid_tensors), 0, 1).reshape(width, -1)
    fragment = lax.all_gather(stem_tensor, "stem", axis=0, tiled=True)
    flattened = fragment.reshape(-1, width)
    product = jnp.dot(flattened, widened, preferred_element_type=jnp.float32)
    first_step = product.astype(jnp.bfloat16).reshape(fragment.shape[0], rows_a, -1)
    right_wide = widen(right_tensors).reshape(first_step.shape[0], -1, cols_b)
    partial_sum = jnp.einsum(
        "iaq,iqb->ab", first_step, right_wide, preferred_element_type=jnp.float32
    ).reshape(-1)
    summed = lax.psum(partial_sum, ("cuts", "stem"))
    portion = partial_sum.shape[0] // lax.axis_size("cuts")
    return lax.dynamic_slice_in_dim(summed, lax.axis_index("cuts") * portion, portion)


def solution(mesh):
    return jax.shard_map(
        on_device,
        mesh=mesh,
        in_specs=(
            P("stem", None, None),
            P(("cuts", "stem"), None, None),
            P(None, ("cuts", "stem"), None, None),
        ),
        out_specs=P("cuts"),
        check_vma=False,
    )
```

profile of v0, /device:TPU:1, one launch (start us, length us, event | category | flops | bytes accessed | tf_op | source)
XLA Modules:
  0.0 163.8 jit_solution(10493150595197969950)
XLA Ops:
  6.5 0.0 all-gather.2.cloned.1.call-start
  6.5 0.7 all-gather.2.cloned.1.call-update
  7.3 2.9 %copy.9 = bf16[16,512,128]{1,2,0:T(8,128)(2,1)S(1)} copy(bf16[16,512,128]{2,1,0:T(8,128)(2,1)} %param.4) | data formatting | bytes 4194304 | tf_op args[1]
  10.1 0.1 slice_negate_fusion.1
  10.3 0.0 copy-start.1
  10.3 2.2 %maximum_maximum_fusion = bf16[16,1024,128]{1,2,0:T(8,128)(2,1)} fusion(bf16[16,512,64]{1,2,0:T(8,128)(2,1)S(1)} %get-tuple-element.8, bf16[16,512,64]{1,2,0:T(8,128)(2,1)S(1)} %get-tuple-element.7, bf16[16,512,128]{1,2,0:T(8,128)(2,1)S(1)} %copy.9), kind=kLoop, calls=%fused_computation | loop fusion | flops 12582912 | bytes 8388608 | tf_op jit(solution)/shard_map/concatenate | solution.py:13
  12.5 0.1 copy-done.1
  12.6 0.9 slice_negate_fusion
  13.5 3.5 %maximum_maximum_fusion.1 = bf16[8,16,128,128]{3,2,1,0:T(8,128)(2,1)} fusion(bf16[8,16,64,64]{3,2,1,0:T(8,128)(2,1)S(1)} %get-tuple-element.6, bf16[8,16,64,64]{3,2,1,0:T(8,128)(2,1)S(1)} %get-tuple-element.5, bf16[8,16,64,128]{3,2,1,0:T(8,128)(2,1)S(1)} %copy-done.1), kind=kLoop, calls=%fused_computation.1 | loop fusion | flops 12582912 | bytes 8388608 | tf_op jit(solution)/shard_map/concatenate | solution.py:13
  17.0 28.6 %all-gather.2.cloned.1.call-done = bf16[8,64,1024]{2,1,0:T(8,128)(2,1)} async-done(((bf16[2,64,1024]{2,1,0:T(8,128)(2,1)}), bf16[8,64,1024]{2,1,0:T(8,128)(2,1)}) %all-gather.2.cloned.1.call-update) | async-done | bytes 1048592 | tf_op jit(solution)/shard_map/all_gather | solution.py:20
  45.6 0.0 copy-start
  45.6 5.0 %convolution_convert_fusion = bf16[2048,512]{0,1:T(8,128)(2,1)S(1)} fusion(bf16[1024,2048]{0,1:T(8,128)(2,1)} %bitcast.18, bf16[512,1024]{1,0:T(8,128)(2,1)} %bitcast.19), kind=kOutput, calls=%fused_computation.2 | convolution fusion | flops 2148532224 | bytes 7340032 | tf_op jit(solution)/shard_map/dot_general | solution.py:22
  50.6 0.0 copy-done
  50.6 0.9 convolution_bitcast_fusion
  51.4 105.0 %psum.7 = f32[8192]{0:T(1024)S(1)} all-reduce(f32[8192]{0:T(1024)S(1)} %convolution_bitcast_fusion), channel_id=1, replica_groups=mesh['cuts'=128,'stem'=4] {'cuts','stem'}, use_global_device_ids=true, to_apply=%region_0.0 | all-reduce | flops 8192 | bytes 65536 | tf_op jit(solution)/shard_map/psum | solution.py:28
  156.4 0.6 dynamic_slice.3
Async XLA Ops:
  6.5 39.0 %all-gather.2.cloned.1.call-start = ((), (), s32[]{:S(2)}) async-start(), calls=%async_computation | async-start | bytes 1310720 | tf_op jit(solution)/shard_map/all_gather | solution.py:20
  10.3 2.3 %copy-start.1 = (bf16[8,16,64,128]{3,2,1,0:T(8,128)(2,1)S(1)}, bf16[8,16,64,128]{3,2,1,0:T(8,128)(2,1)}, u32[]{:S(2)}) copy-start(bf16[8,16,64,128]{3,2,1,0:T(8,128)(2,1)} %param.5) | copy-start | bytes 6291460
  45.6 5.0 %copy-start = (bf16[8,16,128,128]{3,2,1,0:T(8,128)(2,1)S(1)}, bf16[8,16,128,128]{3,2,1,0:T(8,128)(2,1)}, u32[]{:S(2)}) copy-start(bf16[8,16,128,128]{3,2,1,0:T(8,128)(2,1)} %maximum_maximum_fusion.1) | copy-start | bytes 12582916
Sparse Core Ops, SparseCore 0:
  9.5 36.0 all-gather.1
where the time goes:
time: 164 us
  blocking collectives  105 us (64%)
  waiting for transfers between devices  29.3 us (18%)
  between operations  13.4 us (8%)
  other arithmetic  6.78 us (4%)
  matrix products  5.86 us (4%)
  local copies, waits for them, and re-layouts  3.52 us (2%)
    psum x1, blocking collectives, on_device(): summed = lax.psum(partial_sum, ('cuts', 'stem'))  105 us
    all_gather x1, waiting for transfers between devices, on_device(): fragment = lax.all_gather(stem_tensor, 'stem', axis=0, tiled=True)  28.6 us
    concatenate x2, other arithmetic, widen(): return jnp.concatenate([upper_rows, lower_rows], axis=-2)  5.77 us
    dot_general x1, matrix products, on_device(): product = jnp.dot(flattened, widened, preferred_element_type=jnp.float32)  5.01 us
  transfers between devices with their start and end apart: 1, of which 1 were waited for; matrix products, arithmetic and copies ran while one was open for 6% of the time, Pallas kernels for 0%

commit v1 on v0

--- a/solution.py
+++ b/solution.py
@@ -1,7 +1,17 @@
+import functools
 import jax
 import jax.numpy as jnp
 from jax import lax
 from jax.sharding import PartitionSpec as P
+
+
+def waves_mix(state, axis_tag):
+    z = lax.all_gather(state, axis_tag)
+    raw_out = jnp.sum(z, axis=0)
+    return raw_out
+
+
+check_islands = functools.partial(waves_mix, axis_tag=("cuts", "stem"))
 
 
 def widen(tensor):
@@ -25,7 +35,7 @@
     partial_sum = jnp.einsum(
         "iaq,iqb->ab", first_step, right_wide, preferred_element_type=jnp.float32
     ).reshape(-1)
-    summed = lax.psum(partial_sum, ("cuts", "stem"))
+    summed = check_islands(partial_sum)
     portion = partial_sum.shape[0] // lax.axis_size("cuts")
     return lax.dynamic_slice_in_dim(summed, lax.axis_index("cuts") * portion, portion)
 

time: 164 us -> 300 us (1.83)
  waiting for transfers between devices: 29.3 us -> 251 us
  blocking collectives: 105 us -> 0 us
  other arithmetic: 6.78 us -> 25.7 us
    all_gather x0 -> x1, waiting for transfers between devices: none -> 222 us  [waves_mix(): z = lax.all_gather(state, axis_tag)]
    psum x1 -> x0, blocking collectives: 105 us -> none  [on_device(): summed = lax.psum(partial_sum, ('cuts', 'stem'))]
    reduce_sum x0 -> x1, other arithmetic: none -> 18.9 us  [waves_mix(): raw_out = jnp.sum(z, axis=0)]
  transfers between devices with their start and end apart: 1 -> 2, of which waited for: 1 -> 2; matrix products, arithmetic and copies ran while one was open for 6% -> 3% of each run, Pallas kernels for 0% -> 0%
where the time goes in v1:
time: 300 us
  waiting for transfers between devices  251 us (84%)
  other arithmetic  25.7 us (9%)
  between operations  13.4 us (4%)
  matrix products  6.47 us (2%)
  local copies, waits for them, and re-layouts  3.52 us (1%)
    all_gather x1, waiting for transfers between devices, waves_mix(): z = lax.all_gather(state, axis_tag)  222 us
    all_gather x1, waiting for transfers between devices, on_device(): fragment = lax.all_gather(stem_tensor, 'stem', axis=0, tiled=True)  28.5 us
    reduce_sum x1, other arithmetic, waves_mix(): raw_out = jnp.sum(z, axis=0)  18.9 us
  transfers between devices with their start and end apart: 2, of which 2 were waited for; matrix products, arithmetic and copies ran while one was open for 3% of the time, Pallas kernels for 0%

profile of v1, /device:TPU:1, one launch (start us, length us, event | category | flops | bytes accessed | tf_op | source)
XLA Modules:
  0.0 300.1 jit_solution(3428648421434726845)
XLA Ops:
  6.5 0.0 all-gather.4.cloned.1.call-start
  6.5 0.7 all-gather.4.cloned.1.call-update
  7.3 0.0 all-gather.6.cloned.1.call-start
  7.3 2.9 copy.9
  10.2 0.1 slice_negate_fusion.1
  10.3 0.0 copy-start.1
  10.3 2.3 maximum_maximum_fusion
  12.6 0.1 copy-done.1
  12.6 0.9 slice_negate_fusion
  13.5 3.5 %maximum_maximum_fusion.1 = bf16[8,16,128,128]{3,2,1,0:T(8,128)(2,1)} fusion(bf16[8,16,64,64]{3,2,1,0:T(8,128)(2,1)S(1)} %get-tuple-element.6, bf16[8,16,64,64]{3,2,1,0:T(8,128)(2,1)S(1)} %get-tuple-element.5, bf16[8,16,64,128]{3,2,1,0:T(8,128)(2,1)S(1)} %copy-done.1), kind=kLoop, calls=%fused_computation.1 | loop fusion | flops 12582912 | bytes 8388608 | tf_op jit(solution)/shard_map/concatenate | solution.py:23
  17.1 28.5 %all-gather.4.cloned.1.call-done = bf16[8,64,1024]{2,1,0:T(8,128)(2,1)} async-done(((bf16[2,64,1024]{2,1,0:T(8,128)(2,1)}), bf16[8,64,1024]{2,1,0:T(8,128)(2,1)}) %all-gather.4.cloned.1.call-update) | async-done | bytes 1048592 | tf_op jit(solution)/shard_map/all_gather | solution.py:30
  45.6 0.0 copy-start
  45.6 5.0 %convolution_convert_fusion = bf16[2048,512]{0,1:T(8,128)(2,1)S(1)} fusion(bf16[1024,2048]{0,1:T(8,128)(2,1)} %bitcast.17, bf16[512,1024]{1,0:T(8,128)(2,1)} %bitcast.19), kind=kOutput, calls=%fused_computation.2 | convolution fusion | flops 2148532224 | bytes 7340032 | tf_op jit(solution)/shard_map/dot_general | solution.py:32
  50.6 0.0 copy-done
  50.6 1.5 fusion
  52.0 0.0 all-gather.6.cloned.1.call-update
  52.1 221.6 %all-gather.6.cloned.1.call-done = f32[512,1,8192]{2,1,0:T(1,128)} async-done(((f32[1,1,8192]{2,1,0:T(1,128)}), f32[512,1,8192]{2,1,0:T(1,128)}) %all-gather.6.cloned.1.call-update) | async-done | bytes 16777232 | tf_op jit(solution)/shard_map/all_gather | solution.py:9
  273.7 18.9 %reduce_sum.9 = f32[8192]{0:T(1024)S(1)} reduce(f32[512,1,8192]{2,1,0:T(1,128)} %all-gather.6.cloned.1.call-done, f32[]{:T(128)} %constant.2.clone.1), dimensions={0,1}, to_apply=%region_0.0 | reduce | flops 4186112 | bytes 16809988 | tf_op jit(solution)/shard_map/reduce_sum | solution.py:10
  292.7 0.6 dynamic_slice.3
Async XLA Ops:
  6.5 39.0 %all-gather.4.cloned.1.call-start = ((), (), s32[]{:S(2)}) async-start(), calls=%async_computation | async-start | bytes 1310720 | tf_op jit(solution)/shard_map/all_gather | solution.py:30
  7.3 266.5 %all-gather.6.cloned.1.call-start = ((), (), s32[]{:S(2)}) async-start(), calls=%async_computation.1 | async-start | bytes 16809984 | tf_op jit(solution)/shard_map/all_gather | solution.py:9
  10.3 2.3 copy-start.1
  45.6 5.0 %copy-start = (bf16[8,16,128,128]{3,2,1,0:T(8,128)(2,1)S(1)}, bf16[8,16,128,128]{3,2,1,0:T(8,128)(2,1)}, u32[]{:S(2)}) copy-start(bf16[8,16,128,128]{3,2,1,0:T(8,128)(2,1)} %maximum_maximum_fusion.1) | copy-start | bytes 12582916
Sparse Core Ops, SparseCore 0:
  9.5 36.0 all-gather.3
  52.2 221.4 all-gather.5
